TPU v7x, 512 devices: a whole 4x8x8 slice. The times are simulated.
512 devices in a mesh: dp: 64 (over z_hi, x, y), tile: 8 (over z_lo, core).
Axes of the slice: x: 4, y: 8, z: 8 (z_hi: 2, z_lo: 4; z = z_hi * 4 + z_lo), core: 2. Of those that a mesh axis runs over, the one named last changes fastest.
Arguments:
- feats: bfloat16 [4096, 2048], P('dp'), may hold values from -11 to 11
- jitter: bfloat16 [4096, 2048], P('dp'), may hold values from -1.5 to 1.5
- mask_ids: int32 [4096, 2], P('dp'), may hold values from 0 to 31
- proj_weight: bfloat16 [2048, 4096], P('dp', 'tile'), may hold values from -0.125 to 0.125
Outputs:
- feats_grad: float32 [4096, 2048], P('dp', 'tile')
- diag_corr: float32 [4096], P('tile')
- cross_power: float32 [], replicated
All inputs are finite; a program needn't handle non-finite values.
Results may differ from a plain program's by a relative error of at most 0.02.
Values may be sent and summed in bfloat16 or wider, within the bound.
No kernel may reach another device: no remote copies, remote signals or barrier semaphores. Data moves between devices by JAX's collectives and lax.ppermute only.
A program may use at most 64 MiB of HBM per device.

v0:
```python
import jax
import jax.numpy as jnp
from jax import lax
from jax.sharding import PartitionSpec as P

EMB = 4096
GROUPS = 32
LAMBDA_OFF = 0.0051
NORM_EPS = 1e-05
LOSS_SCALE = 65536.0


def masked_views(feats, jitter, mask_ids):
    width = feats.shape[1]
    group_size = width // GROUPS
    channel_group = lax.broadcasted_iota(jnp.int32, (1, width), 1) // group_size
    keep_a = (channel_group != mask_ids[:, 0:1]).astype(jnp.float32)
    keep_b = (channel_group != mask_ids[:, 1:2]).astype(jnp.float32)
    values = feats.astype(jnp.float32)
    view_a = (values * keep_a).astype(jnp.bfloat16)
    view_b = (values * keep_b + jitter.astype(jnp.float32)).astype(jnp.bfloat16)
    return (view_a, view_b, keep_a, keep_b)


def contract_last(left, right):
    return lax.dot_general(
        left, right, (((1,), (1,)), ((), ())), preferred_element_type=jnp.float32
    )


def on_device(feats, jitter, mask_ids, proj_weight):
    view_a, view_b, keep_a, keep_b = masked_views(feats, jitter, mask_ids)
    rows = feats.shape[0]
    total = rows * lax.axis_size("dp")
    piece = lax.all_gather(proj_weight, "dp", axis=0, tiled=True)
    raw_a = jnp.dot(view_a, piece, preferred_element_type=jnp.float32)
    raw_b = jnp.dot(view_b, piece, preferred_element_type=jnp.float32)
    raw_a = raw_a.astype(jnp.bfloat16)
    raw_b = raw_b.astype(jnp.bfloat16)
    values_a = raw_a.astype(jnp.float32)
    values_b = raw_b.astype(jnp.float32)
    moment_sums = lax.psum(
        (
            jnp.sum(values_a, axis=0),
            jnp.sum(values_a * values_a, axis=0),
            jnp.sum(values_b, axis=0),
            jnp.sum(values_b * values_b, axis=0),
        ),
        "dp",
    )
    mean_a = moment_sums[0] / total
    mean_b = moment_sums[2] / total
    inv_a = lax.rsqrt(moment_sums[1] / total - mean_a * mean_a + NORM_EPS)
    inv_b = lax.rsqrt(moment_sums[3] / total - mean_b * mean_b + NORM_EPS)
    norm_a = ((values_a - mean_a) * inv_a).astype(jnp.bfloat16)
    norm_b = ((values_b - mean_b) * inv_b).astype(jnp.bfloat16)
    outgoing_a, outgoing_b = (norm_a, norm_b)
    gathered_a, gathered_b = (
        lax.all_gather(outgoing_a, "dp", axis=0, tiled=True),
        lax.all_gather(outgoing_b, "dp", axis=0, tiled=True),
    )
    whole_a, whole_b = (gathered_a, gathered_b)
    za = norm_a.astype(jnp.float32)
    zb = norm_b.astype(jnp.float32)
    diag_corr = jnp.sum(whole_a.astype(jnp.float32) * whole_b.astype(jnp.float32), axis=0) / total
    gram_a, gram_b = (
        lax.psum(contract_last(norm_a, whole_a).astype(jnp.bfloat16), "tile").astype(jnp.float32),
        lax.psum(contract_last(norm_b, whole_b).astype(jnp.bfloat16), "tile").astype(jnp.float32),
    )
    trace_part = jnp.sum(gram_a * gram_b)
    gram_bf_a = gram_a.astype(jnp.bfloat16)
    gram_bf_b = gram_b.astype(jnp.bfloat16)
    coeff = -2.0 * (1.0 - diag_corr) - 2.0 * LAMBDA_OFF * diag_corr
    factor = 2.0 * LAMBDA_OFF / (total * total)
    grad_na = zb * coeff / total + factor * jnp.dot(
        gram_bf_b, whole_a, preferred_element_type=jnp.float32
    )
    grad_nb = za * coeff / total + factor * jnp.dot(
        gram_bf_a, whole_b, preferred_element_type=jnp.float32
    )
    sums = lax.psum(
        (
            jnp.sum(grad_na, axis=0),
            jnp.sum(grad_na * za, axis=0),
            jnp.sum(grad_nb, axis=0),
            jnp.sum(grad_nb * zb, axis=0),
            trace_part,
        ),
        "dp",
    )
    dz_a = (inv_a * (grad_na - sums[0] / total - za * (sums[1] / total))).astype(jnp.bfloat16)
    dz_b = (inv_b * (grad_nb - sums[2] / total - zb * (sums[3] / total))).astype(jnp.bfloat16)
    cross_power = sums[4] / (total * total) / EMB
    piece = lax.all_gather(proj_weight, "dp", axis=0, tiled=True)
    combined = keep_a * contract_last(dz_a, piece) + keep_b * contract_last(dz_b, piece)
    feats_grad = LOSS_SCALE * lax.psum_scatter(
        combined.astype(jnp.bfloat16), "tile", scatter_dimension=1, tiled=True
    ).astype(jnp.float32)
    return (feats_grad, diag_corr, cross_power)


def solution(mesh):
    in_specs = (P("dp", None), P("dp", None), P("dp", None), P("dp", "tile"))
    out_specs = (P("dp", "tile"), P("tile"), P())
    return jax.shard_map(
        on_device, mesh=mesh, in_specs=in_specs, out_specs=out_specs, check_vma=False
    )
```

profile of v0, /device:TPU:2, one launch (start us, length us, event | category | flops | bytes accessed | tf_op | source)
XLA Modules:
  0.0 1044.2 jit_solution(3339325027411994053)
XLA Ops:
  7.2 0.0 all-gather.4.cloned.1.call-start
  7.2 0.7 all-gather.4.cloned.1.call-update
  7.9 0.0 all-gather.6.cloned.1.call-start
  8.0 0.8 slice_bitcast_fusion
  8.7 147.5 %all-gather.4.cloned.1.call-done = bf16[2048,512]{1,0:T(8,128)(2,1)} async-done(((bf16[32,512]{1,0:T(8,128)(2,1)}), bf16[2048,512]{1,0:T(8,128)(2,1)}) %all-gather.4.cloned.1.call-update) | async-done | bytes 2097168 | tf_op jit(solution)/shard_map/all_gather | solution.py:35
  156.2 2.2 multiply_reduce_fusion.3
  158.5 2.3 fusion.42
  160.8 186.2 %all-reduce.1 = (f32[512]{0:T(512)S(1)}, f32[512]{0:T(512)S(1)}, f32[512]{0:T(512)S(1)}, f32[512]{0:T(512)S(1)}) all-reduce(f32[512]{0:T(512)S(1)} %get-tuple-element.10, f32[512]{0:T(512)S(1)} %get-tuple-element.9, f32[512]{0:T(512)S(1)} %get-tuple-element.8, f32[512]{0:T(512)S(1)} %get-tuple-element.7), channel_id=1, replica_groups=mesh['dp'=64,'tile'=8] {'dp'}, use_global_device_ids=true, to_apply=%region_3.4 | all-reduce | flops 2048 | bytes 16384 | tf_op jit(solution)/shard_map/psum | solution.py:42
  347.0 0.6 multiply_convert_fusion
  347.6 0.0 all-gather.6.cloned.1.call-update
  347.6 0.0 all-gather.8.cloned.1.call-start
  347.7 0.6 multiply_convert_fusion.1
  348.3 0.0 all-gather.8.cloned.1.call-update
  348.4 0.0 all-reduce.5.cloned.1.call-start
  348.4 186.0 %all-gather.6.cloned.1.call-done = bf16[4096,512]{1,0:T(8,128)(2,1)} async-done(((bf16[64,512]{1,0:T(8,128)(2,1)}), bf16[4096,512]{1,0:T(8,128)(2,1)}) %all-gather.6.cloned.1.call-update) | async-done | bytes 4194320 | tf_op jit(solution)/shard_map/all_gather | solution.py:59
  534.4 4.4 convolution_convert_fusion
  538.8 152.4 %all-gather.8.cloned.1.call-done = bf16[4096,512]{1,0:T(8,128)(2,1)} async-done(((bf16[64,512]{1,0:T(8,128)(2,1)}), bf16[4096,512]{1,0:T(8,128)(2,1)}) %all-gather.8.cloned.1.call-update) | async-done | bytes 4194320 | tf_op jit(solution)/shard_map/all_gather | solution.py:60
  691.2 4.4 convolution_convert_fusion.1
  695.6 0.0 all-reduce.5.cloned.1.call-update
  695.6 0.0 reduce-scatter.2.cloned.1.call-start
  695.6 4.6 multiply_reduce_fusion
  700.3 0.6 multiply_subtract_fusion
  700.8 68.8 %all-reduce.5.cloned.1.call-done = (bf16[64,4096]{1,0:T(8,128)(2,1)}, bf16[64,4096]{1,0:T(8,128)(2,1)}) async-done(((bf16[64,4096]{1,0:T(8,128)(2,1)}, bf16[64,4096]{1,0:T(8,128)(2,1)}), (bf16[64,4096]{1,0:T(8,128)(2,1)}, bf16[64,4096]{1,0:T(8,128)(2,1)})) %all-reduce.5.cloned.1.call-update) | async-done | bytes 1048592 | tf_op jit(solution)/shard_map/psum | solution.py:68
  769.7 2.2 multiply_reduce_fusion.1
  771.9 3.4 fusion.40
  775.3 0.9 fusion.41
  776.2 196.4 %all-reduce = (f32[512]{0:T(512)S(1)}, f32[512]{0:T(512)S(1)}, f32[512]{0:T(512)S(1)}, f32[512]{0:T(512)S(1)}, f32[]{:T(128)}) all-reduce(f32[512]{0:T(512)S(1)} %get-tuple-element.6, f32[512]{0:T(512)S(1)} %get-tuple-element.5, f32[512]{0:T(512)S(1)} %get-tuple-element.4, ...), channel_id=1, replica_groups=mesh['dp'=64,'tile'=8] {'dp'}, use_global_device_ids=true, to_apply=%region_13.14 | all-reduce | flops 2049 | bytes 16392 | tf_op jit(solution)/shard_map/psum | solution.py:81
  972.6 0.8 convolution_select_fusion.1
  973.3 1.5 fusion.1
  974.8 0.0 reduce-scatter.2.cloned.1.call-update
  975.4 59.7 %reduce-scatter.2.cloned.1.call-done = bf16[64,256]{1,0:T(8,128)(2,1)} async-done(((bf16[64,2048]{1,0:T(8,128)(2,1)}), bf16[64,256]{1,0:T(8,128)(2,1)}) %reduce-scatter.2.cloned.1.call-update) | async-done | bytes 32784 | tf_op jit(solution)/shard_map/reduce_scatter | solution.py:96
  1035.1 1.4 convert_multiply_fusion.6
  (15 shorter events, 0.0 us)
Async XLA Ops:
  7.2 149.1 %all-gather.4.cloned.1.call-start = ((), (), s32[]{:S(2)}) async-start(), calls=%async_computation.1 | async-start | bytes 2129920 | tf_op jit(solution)/shard_map/all_gather | solution.py:35
  7.9 526.5 %all-gather.6.cloned.1.call-start = ((), (), s32[]{:S(2)}) async-start(), calls=%async_computation.2 | async-start | bytes 4259840 | tf_op jit(solution)/shard_map/all_gather | solution.py:59
  347.6 343.6 %all-gather.8.cloned.1.call-start = ((), (), s32[]{:S(2)}) async-start(), calls=%async_computation.3 | async-start | bytes 4259840 | tf_op jit(solution)/shard_map/all_gather | solution.py:60
  348.3 342.9 %copy-start.3 = (bf16[64,512]{1,0:T(8,128)(2,1)S(1)}, bf16[64,512]{1,0:T(8,128)(2,1)}, u32[]{:S(2)}) copy-start(bf16[64,512]{1,0:T(8,128)(2,1)} %multiply_convert_fusion.1) | copy-start | bytes 196612
  348.4 421.3 %all-reduce.5.cloned.1.call-start = ((), (), s32[]{:S(2)}) async-start(), calls=%async_computation.5 | async-start | bytes 2097152 | tf_op jit(solution)/shard_map/psum | solution.py:68
  695.6 76.3 %copy-start.2 = (bf16[64,512]{1,0:T(8,128)(2,1)S(1)}, bf16[64,512]{1,0:T(8,128)(2,1)}, u32[]{:S(2)}) copy-start(bf16[64,512]{1,0:T(8,128)(2,1)} %multiply_convert_fusion) | copy-start | bytes 196612
  695.6 339.5 %reduce-scatter.2.cloned.1.call-start = ((), (), s32[]{:S(2)}) async-start(), calls=%async_computation.4 | async-start | bytes 294912 | tf_op jit(solution)/shard_map/reduce_scatter | solution.py:96
  769.7 5.6 copy-start
  769.7 5.6 copy-start.4
  771.9 200.6 %copy-start.1 = (bf16[2048,512]{1,0:T(8,128)(2,1)S(1)}, bf16[2048,512]{1,0:T(8,128)(2,1)}, u32[]{:S(2)}) copy-start(bf16[2048,512]{1,0:T(8,128)(2,1)} %all-gather.4.cloned.1.call-done) | copy-start | bytes 6291460
Sparse Core Ops, SparseCore 0:
  12.5 143.6 all-gather.3
  347.7 186.5 all-gather.5
  538.9 152.2 all-gather.7
  695.7 73.9 all-reduce.4
  974.9 60.1 reduce-scatter.1
where the time goes:
time: 1040 us
  waiting for transfers between devices  615 us (59%)
  blocking collectives  383 us (37%)
  matrix products  19.7 us (2%)
  between operations  15.6 us (2%)
    psum x1, blocking collectives, on_device(): lax.psum((jnp.sum(grad_na, axis=0), jnp.sum(grad_na * za, axis=0), jnp.su...  196 us
    psum x1, blocking collectives, on_device(): lax.psum((jnp.sum(values_a, axis=0), jnp.sum(values_a * values_a, axis=0)...  186 us
    all_gather x1, waiting for transfers between devices, on_device(): lax.all_gather(outgoing_a, 'dp', axis=0, tiled=True)  186 us
    all_gather x1, waiting for transfers between devices, on_device(): lax.all_gather(outgoing_b, 'dp', axis=0, tiled=True)  152 us
    all_gather x1, waiting for transfers between devices, on_device(): piece = lax.all_gather(proj_weight, 'dp', axis=0, tiled=True)  148 us
    psum x1, waiting for transfers between devices, on_device(): lax.psum(contract_last(norm_b, whole_b).astype(jnp.bfloat16), 'tile')  68.8 us
    reduce_scatter x1, waiting for transfers between devices, on_device(): lax.psum_scatter(combined.astype(jnp.bfloat16), 'tile', scatter_dimension...  59.7 us
  transfers between devices with their start and end apart: 5, of which 5 were waited for; matrix products, arithmetic and copies ran while one was open for 1% of the time, Pallas kernels for 0%

commit v1 on v0

--- a/solution.py
+++ b/solution.py
@@ -65,7 +65,9 @@
     diag_corr = jnp.sum(whole_a.astype(jnp.float32) * whole_b.astype(jnp.float32), axis=0) / total
     gram_a, gram_b = (
         lax.psum(contract_last(norm_a, whole_a).astype(jnp.bfloat16), "tile").astype(jnp.float32),
-        lax.psum(contract_last(norm_b, whole_b).astype(jnp.bfloat16), "tile").astype(jnp.float32),
+        jnp.sum(
+            lax.all_gather(contract_last(norm_b, whole_b).astype(jnp.bfloat16), "tile"), axis=0
+        ).astype(jnp.float32),
     )
     trace_part = jnp.sum(gram_a * gram_b)
     gram_bf_a = gram_a.astype(jnp.bfloat16)

time: 1040 us -> 1100 us (1.058)
  waiting for transfers between devices: 615 us -> 666 us
    all_gather x0 -> x1, waiting for transfers between devices: none -> 54.9 us  [on_device(): lax.all_gather(contract_last(norm_b, whole_b).astype(jnp.bfloat16), 'tile')]
  transfers between devices with their start and end apart: 5 -> 6, of which waited for: 5 -> 6; matrix products, arithmetic and copies ran while one was open for 1% -> 2% of each run, Pallas kernels for 0% -> 0%
where the time goes in v1:
time: 1100 us
  waiting for transfers between devices  666 us (61%)
  blocking collectives  382 us (35%)
  matrix products  24.4 us (2%)
  between operations  15.9 us (1%)
  other arithmetic  11.8 us (1%)
    psum x1, blocking collectives, on_device(): lax.psum((jnp.sum(grad_na, axis=0), jnp.sum(grad_na * za, axis=0), jnp.su...  196 us
    psum x1, blocking collectives, on_device(): lax.psum((jnp.sum(values_a, axis=0), jnp.sum(values_a * values_a, axis=0)...  186 us
    all_gather x1, waiting for transfers between devices, on_device(): lax.all_gather(outgoing_a, 'dp', axis=0, tiled=True)  186 us
    all_gather x1, waiting for transfers between devices, on_device(): lax.all_gather(outgoing_b, 'dp', axis=0, tiled=True)  152 us
    all_gather x1, waiting for transfers between devices, on_device(): piece = lax.all_gather(proj_weight, 'dp', axis=0, tiled=True)  148 us
    psum x1, waiting for transfers between devices, on_device(): lax.psum(contract_last(norm_a, whole_a).astype(jnp.bfloat16), 'tile')  64.5 us
    reduce_scatter x1, waiting for transfers between devices, on_device(): lax.psum_scatter(combined.astype(jnp.bfloat16), 'tile', scatter_dimension...  60.1 us
    all_gather x1, waiting for transfers between devices, on_device(): lax.all_gather(contract_last(norm_b, whole_b).astype(jnp.bfloat16), 'tile')  54.9 us
  transfers between devices with their start and end apart: 6, of which 6 were waited for; matrix products, arithmetic and copies ran while one was open for 2% of the time, Pallas kernels for 0%

profile of v1, /device:TPU:2, one launch (start us, length us, event | category | flops | bytes accessed | tf_op | source)
XLA Modules:
  0.0 1101.4 jit_solution(14924867659987475729)
XLA Ops:
  7.2 0.0 all-gather.6.cloned.1.call-start
  7.2 0.7 all-gather.6.cloned.1.call-update
  7.9 0.0 all-gather.8.cloned.1.call-start
  8.0 0.8 slice_bitcast_fusion
  8.7 147.5 %all-gather.6.cloned.1.call-done = bf16[2048,512]{1,0:T(8,128)(2,1)} async-done(((bf16[32,512]{1,0:T(8,128)(2,1)}), bf16[2048,512]{1,0:T(8,128)(2,1)}) %all-gather.6.cloned.1.call-update) | async-done | bytes 2097168 | tf_op jit(solution)/shard_map/all_gather | solution.py:35
  156.2 2.2 multiply_reduce_fusion.3
  158.5 2.3 fusion.42
  160.8 186.2 %all-reduce.1 = (f32[512]{0:T(512)S(1)}, f32[512]{0:T(512)S(1)}, f32[512]{0:T(512)S(1)}, f32[512]{0:T(512)S(1)}) all-reduce(f32[512]{0:T(512)S(1)} %get-tuple-element.10, f32[512]{0:T(512)S(1)} %get-tuple-element.9, f32[512]{0:T(512)S(1)} %get-tuple-element.8, f32[512]{0:T(512)S(1)} %get-tuple-element.7), channel_id=1, replica_groups=mesh['dp'=64,'tile'=8] {'dp'}, use_global_device_ids=true, to_apply=%region_3.4 | all-reduce | flops 2048 | bytes 16384 | tf_op jit(solution)/shard_map/psum | solution.py:42
  347.0 0.6 multiply_convert_fusion
  347.6 0.0 all-gather.10.cloned.1.call-start
  347.7 0.6 multiply_convert_fusion.1
  348.3 0.0 all-gather.10.cloned.1.call-update
  348.4 0.0 all-reduce.4.cloned.1.call-start
  348.4 186.0 %all-gather.8.cloned.1.call-done = bf16[4096,512]{1,0:T(8,128)(2,1)} async-done(((bf16[64,512]{1,0:T(8,128)(2,1)}), bf16[4096,512]{1,0:T(8,128)(2,1)}) %all-gather.8.cloned.1.call-update) | async-done | bytes 4194320 | tf_op jit(solution)/shard_map/all_gather | solution.py:59
  534.4 4.4 convolution_convert_fusion
  538.8 0.0 all-gather.12.cloned.1.call-start
  538.9 152.3 %all-gather.10.cloned.1.call-done = bf16[4096,512]{1,0:T(8,128)(2,1)} async-done(((bf16[64,512]{1,0:T(8,128)(2,1)}), bf16[4096,512]{1,0:T(8,128)(2,1)}) %all-gather.10.cloned.1.call-update) | async-done | bytes 4194320 | tf_op jit(solution)/shard_map/all_gather | solution.py:60
  691.2 4.4 convolution_convert_fusion.1
  695.6 0.0 reduce-scatter.2.cloned.1.call-start
  695.7 4.6 multiply_reduce_fusion
  700.3 0.6 multiply_subtract_fusion
  700.9 64.5 %all-reduce.4.cloned.1.call-done = bf16[64,4096]{1,0:T(8,128)(2,1)} async-done(((bf16[64,4096]{1,0:T(8,128)(2,1)}), bf16[64,4096]{1,0:T(8,128)(2,1)}) %all-reduce.4.cloned.1.call-update) | async-done | bytes 524304 | tf_op jit(solution)/shard_map/psum | solution.py:67
  765.3 3.8 fusion.40
  769.1 54.9 %all-gather.12.cloned.1.call-done = bf16[512,4096]{1,0:T(8,128)(2,1)} async-done(((bf16[64,4096]{1,0:T(8,128)(2,1)}), bf16[512,4096]{1,0:T(8,128)(2,1)}) %all-gather.12.cloned.1.call-update) | async-done | bytes 4194320 | tf_op jit(solution)/shard_map/all_gather | solution.py:69
  824.1 3.0 reduce_sum.107
  827.1 3.8 fusion.41
  830.9 0.9 multiply_reduce_fusion.1
  831.8 196.1 %all-reduce = (f32[512]{0:T(512)S(1)}, f32[512]{0:T(512)S(1)}, f32[512]{0:T(512)S(1)}, f32[512]{0:T(512)S(1)}, f32[]{:T(128)}) all-reduce(f32[512]{0:T(512)} %get-tuple-element.6, f32[512]{0:T(512)} %get-tuple-element.5, f32[512]{0:T(512)} %get-tuple-element.4, f32[512]{0:T(512)} %get-tuple-element.3, ...), channel_id=1, replica_groups=mesh['dp'=64,'tile'=8] {'dp'}, use_global_device_ids=true, to_apply=%region_13.14 | all-reduce | flops 2049 | bytes 16392 | tf_op jit(solution)/shard_map/psum | solution.py:83
  1027.9 1.4 convolution_select_fusion.1
  1029.3 2.1 fusion.1
  1032.0 60.1 %reduce-scatter.2.cloned.1.call-done = bf16[64,256]{1,0:T(8,128)(2,1)} async-done(((bf16[64,2048]{1,0:T(8,128)(2,1)}), bf16[64,256]{1,0:T(8,128)(2,1)}) %reduce-scatter.2.cloned.1.call-update) | async-done | bytes 32784 | tf_op jit(solution)/shard_map/reduce_scatter | solution.py:98
  1092.1 1.4 convert_multiply_fusion.6
  (23 shorter events, 0.1 us)
Async XLA Ops:
  7.2 149.1 %all-gather.6.cloned.1.call-start = ((), (), s32[]{:S(2)}) async-start(), calls=%async_computation.1 | async-start | bytes 2129920 | tf_op jit(solution)/shard_map/all_gather | solution.py:35
  7.9 526.5 %all-gather.8.cloned.1.call-start = ((), (), s32[]{:S(2)}) async-start(), calls=%async_computation.2 | async-start | bytes 4259840 | tf_op jit(solution)/shard_map/all_gather | solution.py:59
  8.7 149.8 %copy-start.6 = (s32[64]{0:T(128)}, s32[64]{0:T(128)S(1)}, u32[]{:S(2)}) copy-start(s32[64]{0:T(128)S(1)} %get-tuple-element.27) | copy-start | bytes 772
  8.7 530.1 %copy-start.5 = (s32[64]{0:T(128)}, s32[64]{0:T(128)S(1)}, u32[]{:S(2)}) copy-start(s32[64]{0:T(128)S(1)} %get-tuple-element.26) | copy-start | bytes 772
  347.6 343.6 %all-gather.10.cloned.1.call-start = ((), (), s32[]{:S(2)}) async-start(), calls=%async_computation.3 | async-start | bytes 4259840 | tf_op jit(solution)/shard_map/all_gather | solution.py:60
  347.7 347.9 %copy-start.4 = (f32[512]{0:T(512)}, f32[512]{0:T(512)S(1)}, u32[]{:S(2)}) copy-start(f32[512]{0:T(512)S(1)} %get-tuple-element.23) | copy-start | bytes 6148
  348.3 342.9 %copy-start.2 = (bf16[64,512]{1,0:T(8,128)(2,1)S(1)}, bf16[64,512]{1,0:T(8,128)(2,1)}, u32[]{:S(2)}) copy-start(bf16[64,512]{1,0:T(8,128)(2,1)} %multiply_convert_fusion.1) | copy-start | bytes 196612
  348.4 417.0 %all-reduce.4.cloned.1.call-start = ((), (), s32[]{:S(2)}) async-start(), calls=%async_computation.4 | async-start | bytes 1048576 | tf_op jit(solution)/shard_map/psum | solution.py:67
  538.8 285.3 %all-gather.12.cloned.1.call-start = ((), (), s32[]{:S(2)}) async-start(), calls=%async_computation.6 | async-start | bytes 4718592 | tf_op jit(solution)/shard_map/all_gather | solution.py:69
  695.6 69.7 %copy-start.1 = (bf16[64,512]{1,0:T(8,128)(2,1)S(1)}, bf16[64,512]{1,0:T(8,128)(2,1)}, u32[]{:S(2)}) copy-start(bf16[64,512]{1,0:T(8,128)(2,1)} %multiply_convert_fusion) | copy-start | bytes 196612
  695.6 396.5 %reduce-scatter.2.cloned.1.call-start = ((), (), s32[]{:S(2)}) async-start(), calls=%async_computation.5 | async-start | bytes 294912 | tf_op jit(solution)/shard_map/reduce_scatter | solution.py:98
  824.1 6.8 copy-start.3
  827.1 200.8 %copy-start = (bf16[2048,512]{1,0:T(8,128)(2,1)S(1)}, bf16[2048,512]{1,0:T(8,128)(2,1)}, u32[]{:S(2)}) copy-start(bf16[2048,512]{1,0:T(8,128)(2,1)} %all-gather.6.cloned.1.call-done) | copy-start | bytes 6291460
Sparse Core Ops, SparseCore 0:
  12.5 143.6 all-gather.5
  347.8 186.5 all-gather.7
  538.9 152.2 all-gather.9
  694.0 71.3 all-reduce.3
  767.5 56.5 all-gather.11
  1031.5 60.5 reduce-scatter.1
